TPU v7x, 32 devices: a whole 2x2x4 slice. The times are simulated.
32 devices in a mesh: var: 4 (over x, core), space: 8 (over z, y).
Axes of the slice: x: 2, y: 2, z: 4, core: 2. Of those that a mesh axis runs over, the one named last changes fastest.
Arguments:
- fields: bfloat16 [8, 1024, 32768], P('var', None, 'space'), may hold values from -6 to 6
- eigenfunctions: bfloat16 [8, 64, 32768], P('var', None, 'space'), may hold values from -0.03125 to 0.03125
- start: float32 [512, 128], replicated, may hold values from -6 to 6
- grid_count: int32 [8], replicated, may hold values from 16384 to 32768
Outputs:
- loadings: bfloat16 [8, 128, 32768], P('var', None, 'space')
- component_scores: float32 [1024, 128], replicated
- explained: float32 [8, 1024], P('var')
Inputs may be any that keep to these rules, and one draw needn't show every extreme that they name: The grid of variable v is its points 0 to grid_count[v] - 1.
All inputs are finite; a program needn't handle non-finite values.
Results may differ from a plain program's by a relative error of at most 0.005.
Values sent between devices are 32-bit elements; how exact they have to be, the bound alone decides.
A program may use at most 64 MiB of HBM per device.

v0:
```python
import jax
import jax.numpy as jnp
from jax import lax
from jax.sharding import PartitionSpec as P

M = 64
SWEEPS = 2


def orthogonalize(image, gram):
    lower = jnp.linalg.cholesky(gram)
    return jax.scipy.linalg.solve_triangular(lower, image.T, lower=True).T


def product(left, right):
    return jnp.dot(left, right, precision=lax.Precision.HIGHEST, preferred_element_type=jnp.float32)


def shards(fields, eigenfunctions, start, grid_count):
    local_vars, samples, local_points = fields.shape
    first_var = lax.axis_index("var") * local_vars
    counts = lax.dynamic_slice_in_dim(grid_count, first_var, local_vars, 0)
    points = lax.axis_index("space") * local_points + jnp.arange(local_points, dtype=jnp.int32)
    valid = points[None, :] < counts[:, None]
    masked = jnp.where(valid[:, None, :], eigenfunctions, jnp.zeros((), eigenfunctions.dtype))
    part = jnp.einsum("vng,vmg->nvm", fields, masked, preferred_element_type=jnp.float32)
    summed = lax.psum(part.reshape(samples, local_vars * M), "space")
    joint = lax.all_gather(summed, "var", axis=1, tiled=True)
    centred = joint - jnp.mean(joint, axis=0, keepdims=True)
    basis = start
    cov = product(centred.T, centred) / (samples - 1)
    for sweep in range(SWEEPS):
        image = product(cov, basis)
        basis = orthogonalize(image, product(image.T, image))
    component_scores = product(centred, basis)
    scores_low = component_scores.astype(jnp.bfloat16)
    own_basis = lax.dynamic_slice_in_dim(basis, first_var * M, local_vars * M, 0)
    basis_low = own_basis.astype(jnp.bfloat16).reshape(local_vars, M, basis.shape[1])
    loadings = jnp.einsum(
        "vmk,vmg->vkg", basis_low, masked, preferred_element_type=jnp.float32
    ).astype(jnp.bfloat16)
    partial_gain = []
    for local in range(local_vars):
        rebuilt = jnp.dot(scores_low, loadings[local], preferred_element_type=jnp.float32)
        wide = fields[local].astype(jnp.float32)
        deviation = wide - jnp.mean(wide, axis=0, keepdims=True)
        partial_gain.append(jnp.sum(2.0 * deviation * rebuilt - rebuilt * rebuilt, axis=1) / M)
    explained = lax.psum(jnp.stack(partial_gain, axis=0), "space")
    return (loadings, component_scores, explained)


def solution(mesh):
    return jax.shard_map(
        shards,
        mesh=mesh,
        in_specs=(P("var", None, "space"), P("var", None, "space"), P(), P()),
        out_specs=(P("var", None, "space"), P(), P("var", None)),
        check_vma=False,
    )
```

profile of v0, /device:TPU:0, one launch (start us, length us, event | category | flops | bytes accessed | tf_op | source)
XLA Modules:
  0.0 234.2 jit_solution(11181255422536817181)
XLA Ops:
  7.2 0.0 copy-start
  7.2 0.0 all-reduce.2.cloned.1.call-start
  7.2 0.7 dynamic_slice.6
  8.0 0.1 broadcast_compare_fusion
  8.1 12.1 %fusion.19 = f32[2,64,1024]{2,1,0:T(8,128)} fusion(bf16[2,1024,4096]{2,1,0:T(8,128)(2,1)} %param.7, bf16[2,64,4096]{2,1,0:T(8,128)(2,1)} %param.8, pred[2,4096]{1,0:T(4,128)(4,1)S(1)} %broadcast_compare_fusion), kind=kOutput, calls=%fused_computation.25 | convolution fusion | flops 1074266112 | bytes 18358272 | tf_op jit(solution)/shard_map/vng,vmg->nvm/dot_general | solution.py:26
  20.2 0.0 all-reduce.2.cloned.1.call-update
  20.2 0.0 all-gather.2.cloned.1.call-start
  20.2 75.6 %all-reduce.2.cloned.1.call-done = f32[1024,128]{0,1:T(8,128)} async-done(((f32[1024,128]{0,1:T(8,128)}), f32[1024,128]{0,1:T(8,128)}) %all-reduce.2.cloned.1.call-update) | async-done | bytes 524304 | tf_op jit(solution)/shard_map/psum | solution.py:27
  95.8 0.0 all-gather.2.cloned.1.call-update
  95.9 7.8 %convert_reduce_fusion.1 = (f32[4096]{0:T(1024)S(1)}, f32[4096]{0:T(1024)S(1)}) fusion(bf16[2,1024,4096]{2,1,0:T(8,128)(2,1)} %param.7), kind=kLoop, calls=%fused_computation.2 | loop fusion | flops 16769024 | bytes 16809984 | tf_op jit(solution)/shard_map/reduce_sum | solution.py:46
  103.6 0.6 broadcast_multiply_fusion
  104.2 14.9 %all-gather.2.cloned.1.call-done = f32[1024,512]{0,1:T(8,128)} async-done(((f32[1024,128]{0,1:T(8,128)}), f32[1024,512]{0,1:T(8,128)}) %all-gather.2.cloned.1.call-update) | async-done | bytes 2097168 | tf_op jit(solution)/shard_map/all_gather | solution.py:28
  119.2 1.9 reduce_sum.45
  121.1 0.0 copy-start.10
  121.1 5.9 %fusion.14 = f32[512,512]{1,0:T(8,128)S(1)} fusion(f32[1024,512]{0,1:T(8,128)} %all-gather.2.cloned.1.call-done, f32[512]{0:T(512)S(1)} %broadcast_multiply_fusion.4), kind=kOutput, calls=%fused_computation.19 | convolution fusion | flops 3222011904 | bytes 3147776 | tf_op jit(solution)/shard_map/dot_general | solution.py:16
  127.0 1.0 copy-done.3
  128.0 1.0 fusion.39
  129.0 0.7 copy-done.5
  129.7 0.6 fusion.40
  130.3 0.1 copy.10
  130.4 0.6 fusion.33
  131.0 12.5 %cholesky.44 = f32[128,128]{1,0:T(8,128)S(1)} custom-call(f32[128,128]{1,0:T(8,128)} %fusion.33), custom_call_target="Cholesky" | custom-call | tf_op jit(solution)/shard_map/jit(cholesky)/cholesky | solution.py:11
  143.6 0.6 compare_reduce_fusion.1
  144.3 0.6 fusion.28
  144.9 9.8 %custom-call.6 = f32[1,128,128]{1,2,0:T(8,128)S(1)} custom-call(f32[1,128,128]{2,1,0:T(8,128)S(1)} %fusion.28), custom_call_target="InvertDiagBlocksLowerTriangular" | custom-call | tf_op jit(solution)/shard_map/jit(_solve_triangular)/triangular_solve | solution.py:12
  154.7 1.4 fusion.24
  156.1 2.5 %fusion.41 = f32[512,128]{1,0:T(8,128)S(1)} fusion(f32[512,512]{1,0:T(8,128)} %copy-done.3, f32[128,512]{1,0:T(8,128)S(1)} %fusion.24), kind=kOutput, calls=%fused_computation.65 | convolution fusion | flops 402653184 | bytes 1572864 | tf_op jit(solution)/shard_map/dot_general | solution.py:16
  158.6 0.0 copy-start.4
  158.6 0.7 copy-done.4
  159.3 0.6 fusion.42
  159.9 0.1 copy.11
  160.0 0.6 fusion.31
  160.6 12.5 %cholesky.55 = f32[128,128]{1,0:T(8,128)S(1)} custom-call(f32[128,128]{1,0:T(8,128)} %fusion.31), custom_call_target="Cholesky" | custom-call | tf_op jit(solution)/shard_map/jit(cholesky)/cholesky | solution.py:11
  173.2 0.6 compare_reduce_fusion
  173.8 0.7 fusion.29
  174.5 9.8 %custom-call.7 = f32[1,128,128]{1,2,0:T(8,128)S(1)} custom-call(f32[1,128,128]{2,1,0:T(8,128)S(1)} %fusion.29), custom_call_target="InvertDiagBlocksLowerTriangular" | custom-call | tf_op jit(solution)/shard_map/jit(_solve_triangular)/triangular_solve | solution.py:12
  184.3 1.4 fusion.22
  185.7 0.0 copy-start.7
  185.7 0.7 copy-done.7
  186.4 0.1 copy.12
  186.5 0.8 convolution_convert_fusion
  187.3 4.7 %fusion.10 = f32[1024,128]{1,0:T(8,128)S(1)} fusion(f32[128,512]{1,0:T(8,128)} %copy-done.7, f32[1024,512]{0,1:T(8,128)S(1)} %copy-done.2, f32[512]{0:T(512)} %copy-done.10), kind=kOutput, calls=%fused_computation.15 | convolution fusion | flops 805830656 | bytes 2885632 | tf_op jit(solution)/shard_map/dot_general | solution.py:16
  192.0 0.0 slice-start
  192.1 7.2 %fusion.9 = f32[1024]{0:T(1024)S(1)} fusion(f32[4096]{0:T(1024)} %get-tuple-element.7, bf16[2,1024,4096]{2,1,0:T(8,128)(2,1)} %param.7, bf16[2,128,4096]{2,1,0:T(8,128)(2,1)S(1)} %convolution_convert_fusion, f32[1024,128]{1,0:T(8,128)S(1)} %fusion.10), kind=kOutput, calls=%fused_computation.13 | convolution fusion | flops 1103232000 | bytes 9981952 | tf_op jit(solution)/shard_map/dot_general | solution.py:44
  199.3 0.0 slice-done.2
  199.4 1.2 slice-done.3
  200.5 4.5 %fusion.4 = f32[1024]{0:T(1024)S(1)} fusion(f32[4096]{0:T(1024)S(1)} %copy-done.9, bf16[2,1024,4096]{2,1,0:T(8,128)(2,1)S(1)} %bitcast.74, bf16[2,128,4096]{2,1,0:T(8,128)(2,1)S(1)} %convolution_convert_fusion, f32[1024,128]{1,0:T(8,128)S(1)} %fusion.10), kind=kOutput, calls=%fused_computation.8 | convolution fusion | flops 1103232000 | bytes 9981952 | tf_op jit(solution)/shard_map/dot_general | solution.py:44
  205.2 22.2 %psum.15 = f32[2,1024]{1,0:T(2,128)} all-reduce(f32[2,1024]{1,0:T(2,128)S(1)} %pad_maximum_fusion), channel_id=1, replica_groups=mesh['var'=4,'space'=8] {'space'}, use_global_device_ids=true, to_apply=%region_8.11 | all-reduce | flops 2048 | bytes 16384 | tf_op jit(solution)/shard_map/psum | solution.py:48
  (28 shorter events, 0.2 us)
Async XLA Ops:
  7.2 120.8 %copy-start = (f32[512,128]{1,0:T(8,128)S(1)}, f32[512,128]{1,0:T(8,128)}, u32[]{:S(2)}) copy-start(f32[512,128]{1,0:T(8,128)} %param.9) | copy-start | bytes 786436
  7.2 88.6 %all-reduce.2.cloned.1.call-start = ((), (), s32[]{:S(2)}) async-start(), calls=%async_computation | async-start | bytes 1048576 | tf_op jit(solution)/shard_map/psum | solution.py:27
  20.2 166.4 %copy-start.1 = (bf16[2,64,4096]{2,1,0:T(8,128)(2,1)S(1)}, bf16[2,64,4096]{2,1,0:T(8,128)(2,1)}, u32[]{:S(2)}) copy-start(bf16[2,64,4096]{2,1,0:T(8,128)(2,1)} %param.8) | copy-start | bytes 3145732
  20.2 99.0 %all-gather.2.cloned.1.call-start = ((), (), s32[]{:S(2)}) async-start(), calls=%async_computation.1 | async-start | bytes 2621440 | tf_op jit(solution)/shard_map/all_gather | solution.py:28
  119.2 68.1 %copy-start.2 = (f32[1024,512]{0,1:T(8,128)S(1)}, f32[1024,512]{0,1:T(8,128)}, u32[]{:S(2)}) copy-start(f32[1024,512]{0,1:T(8,128)} %all-gather.2.cloned.1.call-done) | copy-start | bytes 6291460
  121.1 5.9 %copy-start.10 = (f32[512]{0:T(512)}, f32[512]{0:T(512)S(1)}, u32[]{:S(2)}) copy-start(f32[512]{0:T(512)S(1)} %broadcast_multiply_fusion.4) | copy-start | bytes 6148
  127.0 1.0 copy-start.3
  129.0 0.7 copy-start.5
  158.6 0.7 copy-start.4
  185.7 0.7 copy-start.7
  187.3 12.0 %copy-start.6 = (bf16[2,128,4096]{2,1,0:T(8,128)(2,1)}, bf16[2,128,4096]{2,1,0:T(8,128)(2,1)S(1)}, u32[]{:S(2)}) copy-start(bf16[2,128,4096]{2,1,0:T(8,128)(2,1)S(1)} %convolution_convert_fusion) | copy-start | bytes 6291460
  192.0 13.1 %copy-start.8 = (f32[1024,128]{1,0:T(8,128)}, f32[1024,128]{1,0:T(8,128)S(1)}, u32[]{:S(2)}) copy-start(f32[1024,128]{1,0:T(8,128)S(1)} %fusion.10) | copy-start | bytes 1572868
  192.0 7.3 %slice-start = ((s8[16777216]{0:T(1024)(128)(4,1)}), s8[4194304]{0:T(1024)(128)(4,1)S(1)}, s32[]{:S(2)}) async-start(s8[16777216]{0:T(1024)(128)(4,1)} %bitcast.73), calls=%async_computation.2 | async-start | bytes 8388608
  192.0 7.3 %copy-start.9 = (f32[4096]{0:T(1024)S(1)}, f32[4096]{0:T(1024)}, u32[]{:S(2)}) copy-start(f32[4096]{0:T(1024)} %get-tuple-element.8) | copy-start | bytes 49156
  192.0 7.3 %slice-start.1 = ((s8[16777216]{0:T(1024)(128)(4,1)}), s8[4194304]{0:T(1024)(128)(4,1)S(1)}, s32[]{:S(2)}) async-start(s8[16777216]{0:T(1024)(128)(4,1)} %bitcast.73), calls=%async_computation.3 | async-start | bytes 8388608
  192.1 7.3 %slice-start.2 = ((s8[16777216]{0:T(1024)(128)(4,1)}), s8[4194304]{0:T(1024)(128)(4,1)S(1)}, s32[]{:S(2)}) async-start(s8[16777216]{0:T(1024)(128)(4,1)} %bitcast.73), calls=%async_computation.4 | async-start | bytes 8388608
  192.1 8.5 %slice-start.3 = ((s8[16777216]{0:T(1024)(128)(4,1)}), s8[4194304]{0:T(1024)(128)(4,1)S(1)}, s32[]{:S(2)}) async-start(s8[16777216]{0:T(1024)(128)(4,1)} %bitcast.73), calls=%async_computation.5 | async-start | bytes 8388608
Sparse Core Ops, SparseCore 0:
  20.3 75.4 all-reduce.1
  97.4 21.7 all-gather.1
where the time goes:
time: 235 us; the launch traced here: 234 us
  waiting for transfers between devices  90.5 us (39%)
  other arithmetic  59 us (25%)
  matrix products  42.6 us (18%)
  blocking collectives  22.2 us (9%)
  between operations  14.4 us (6%)
  local copies, waits for them, and re-layouts  5.37 us (2%)
    psum x1, waiting for transfers between devices, shards(): summed = lax.psum(part.reshape(samples, local_vars * M), 'space')  75.6 us
    another operation x6, other arithmetic, orthogonalize(): lower = jnp.linalg.cholesky(gram)  26.4 us
    psum x1, blocking collectives, shards(): explained = lax.psum(jnp.stack(partial_gain, axis=0), 'space')  22.2 us
    another operation x4, other arithmetic, orthogonalize(): return jax.scipy.linalg.solve_triangular(lower, image.T, lower=True).T  20.9 us
    dot_general x6, matrix products, product(): jnp.dot(left, right, precision=lax.Precision.HIGHEST, preferred_element_t...  15.2 us
    all_gather x1, waiting for transfers between devices, shards(): joint = lax.all_gather(summed, 'var', axis=1, tiled=True)  14.9 us
    dot_general x1, matrix products, shards(): jnp.einsum('vng,vmg->nvm', fields, masked, preferred_element_type=jnp.flo...  12.1 us
    dot_general x2, matrix products, shards(): jnp.dot(scores_low, loadings[local], preferred_element_type=jnp.float32)  11.8 us
  transfers between devices with their start and end apart: 2, of which 2 were waited for; matrix products, arithmetic and copies ran while one was open for 4% of the time, Pallas kernels for 0%

commit v1 on v0

--- a/solution.py
+++ b/solution.py
@@ -25,7 +25,14 @@
     masked = jnp.where(valid[:, None, :], eigenfunctions, jnp.zeros((), eigenfunctions.dtype))
     part = jnp.einsum("vng,vmg->nvm", fields, masked, preferred_element_type=jnp.float32)
     summed = lax.psum(part.reshape(samples, local_vars * M), "space")
-    joint = lax.all_gather(summed, "var", axis=1, tiled=True)
+    size = lax.axis_size("var")
+    route = [(i, (i + 1) % size) for i in range(size)]
+    parts = [summed]
+    for far in range(1, size):
+        parts = [lax.ppermute(parts[0], "var", route), *parts]
+    whole = jnp.concatenate(parts, axis=1)
+    shift = (lax.axis_index("var") + 1) * parts[-1].shape[1]
+    joint = jnp.roll(whole, shift, axis=1)
     centred = joint - jnp.mean(joint, axis=0, keepdims=True)
     basis = start
     cov = product(centred.T, centred) / (samples - 1)

time: 235 us -> 223 us (0.949)
  other arithmetic: 59 us -> 53.8 us
  matrix products: 42.6 us -> 38.6 us
  local copies, waits for them, and re-layouts: 5.37 us -> 1.48 us
  waiting for transfers between devices: 90.5 us -> 93.8 us
    ppermute x0 -> x3, waiting for transfers between devices: none -> 18.2 us  [shards(): parts = [lax.ppermute(parts[0], 'var', route), *parts]]
    all_gather x1 -> x0, waiting for transfers between devices: 14.9 us -> none  [shards(): joint = lax.all_gather(summed, 'var', axis=1, tiled=True)]
    unnamed x30 -> x27, local copies, waits for them, and re-layouts: 4.33 us -> 0.4 us
    dot_general x6, matrix products: 15.2 us -> 12.2 us  [product(): jnp.dot(left, right, precision=lax.Precision.HIGHEST, preferred_element_t...]
  transfers between devices with their start and end apart: 2 -> 4, of which waited for: 2 -> 4; matrix products, arithmetic and copies ran while one was open for 4% -> 3% of each run, Pallas kernels for 0% -> 0%
where the time goes in v1:
time: 223 us
  waiting for transfers between devices  93.8 us (42%)
  other arithmetic  53.8 us (24%)
  matrix products  38.6 us (17%)
  blocking collectives  20.5 us (9%)
  between operations  14.5 us (7%)
    psum x1, waiting for transfers between devices, shards(): summed = lax.psum(part.reshape(samples, local_vars * M), 'space')  75.6 us
    another operation x6, other arithmetic, orthogonalize(): lower = jnp.linalg.cholesky(gram)  24.8 us
    another operation x4, other arithmetic, orthogonalize(): return jax.scipy.linalg.solve_triangular(lower, image.T, lower=True).T  20.9 us
    psum x1, blocking collectives, shards(): explained = lax.psum(jnp.stack(partial_gain, axis=0), 'space')  20.5 us
    ppermute x3, waiting for transfers between devices, shards(): parts = [lax.ppermute(parts[0], 'var', route), *parts]  18.2 us
    dot_general x2, matrix products, shards(): jnp.dot(scores_low, loadings[local], preferred_element_type=jnp.float32)  12.7 us
    dot_general x6, matrix products, product(): jnp.dot(left, right, precision=lax.Precision.HIGHEST, preferred_element_t...  12.2 us
    dot_general x1, matrix products, shards(): jnp.einsum('vng,vmg->nvm', fields, masked, preferred_element_type=jnp.flo...  12.1 us
  transfers between devices with their start and end apart: 4, of which 4 were waited for; matrix products, arithmetic and copies ran while one was open for 3% of the time, Pallas kernels for 0%

profile of v1, /device:TPU:0, one launch (start us, length us, event | category | flops | bytes accessed | tf_op | source)
XLA Modules:
  0.0 222.6 jit_solution(18258958401412189234)
XLA Ops:
  7.2 0.0 copy-start
  7.2 0.0 all-reduce.2.cloned.1.call-start
  7.2 0.7 dynamic_slice.10
  8.0 0.1 broadcast_compare_fusion
  8.1 12.1 %fusion.21 = f32[2,64,1024]{2,1,0:T(8,128)} fusion(bf16[2,1024,4096]{2,1,0:T(8,128)(2,1)} %param.7, bf16[2,64,4096]{2,1,0:T(8,128)(2,1)} %param.8, pred[2,4096]{1,0:T(4,128)(4,1)S(1)} %broadcast_compare_fusion), kind=kOutput, calls=%fused_computation.28 | convolution fusion | flops 1074266112 | bytes 18358272 | tf_op jit(solution)/shard_map/vng,vmg->nvm/dot_general | solution.py:26
  20.2 0.0 all-reduce.2.cloned.1.call-update
  20.2 75.6 %all-reduce.2.cloned.1.call-done = f32[1024,128]{0,1:T(8,128)} async-done(((f32[1024,128]{0,1:T(8,128)}), f32[1024,128]{0,1:T(8,128)}) %all-reduce.2.cloned.1.call-update) | async-done | bytes 524304 | tf_op jit(solution)/shard_map/psum | solution.py:27
  95.8 0.0 collective-permute-start
  95.8 8.8 %collective-permute-done = f32[1024,128]{0,1:T(8,128)S(1)} collective-permute-done((f32[1024,128]{0,1:T(8,128)}, f32[1024,128]{0,1:T(8,128)S(1)}, u32[]{:S(2)}, u32[]{:S(2)}) %collective-permute-start) | collective-permute-done | bytes 524320 | tf_op jit(solution)/shard_map/ppermute | solution.py:32
  104.6 0.0 collective-permute-start.1
  104.6 8.6 %collective-permute-done.1 = f32[1024,128]{0,1:T(8,128)S(1)} collective-permute-done((f32[1024,128]{0,1:T(8,128)S(1)}, f32[1024,128]{0,1:T(8,128)S(1)}, u32[]{:S(2)}, u32[]{:S(2)}) %collective-permute-start.1) | collective-permute-done | bytes 524320 | tf_op jit(solution)/shard_map/ppermute | solution.py:32
  113.2 0.0 collective-permute-start.2
  113.2 7.8 %convert_reduce_fusion.1 = (f32[4096]{0:T(1024)S(1)}, f32[4096]{0:T(1024)S(1)}) fusion(bf16[2,1024,4096]{2,1,0:T(8,128)(2,1)} %param.7), kind=kLoop, calls=%fused_computation.2 | loop fusion | flops 16769024 | bytes 16809984 | tf_op jit(solution)/shard_map/reduce_sum | solution.py:53
  121.0 0.8 collective-permute-done.2
  122.2 0.2 dynamic-slice_reduce_fusion
  122.4 3.7 %fusion.16 = f32[512,512]{1,0:T(8,128)S(1)} fusion(f32[1024,1024]{0,1:T(8,128)S(1)} %constant_dynamic-update-slice_fusion, s32[]{:T(128)S(6)} %select_n.29, f32[512]{0:T(512)S(1)} %broadcast_multiply_fusion.4), kind=kOutput, calls=%fused_computation.22 | convolution fusion | flops 3222011904 | bytes 3147780 | tf_op jit(solution)/shard_map/dot_general | solution.py:16
  126.1 1.0 fusion.43
  127.1 0.0 copy-start.1
  127.1 0.6 fusion.44
  127.7 0.1 copy.10
  127.8 11.7 %cholesky.44 = f32[128,128]{1,0:T(8,128)S(1)} custom-call(f32[128,128]{1,0:T(8,128)S(1)} %fusion.35), custom_call_target="Cholesky" | custom-call | tf_op jit(solution)/shard_map/jit(cholesky)/cholesky | solution.py:11
  139.6 0.6 compare_reduce_fusion.1
  140.2 0.7 fusion.30
  140.9 9.8 %custom-call.6 = f32[1,128,128]{1,2,0:T(8,128)S(1)} custom-call(f32[1,128,128]{2,1,0:T(8,128)S(1)} %fusion.30), custom_call_target="InvertDiagBlocksLowerTriangular" | custom-call | tf_op jit(solution)/shard_map/jit(_solve_triangular)/triangular_solve | solution.py:12
  150.7 0.4 fusion.26
  151.1 1.2 fusion.45
  152.4 0.6 fusion.46
  153.0 0.1 copy.11
  153.1 11.7 %cholesky.55 = f32[128,128]{1,0:T(8,128)S(1)} custom-call(f32[128,128]{1,0:T(8,128)S(1)} %fusion.33), custom_call_target="Cholesky" | custom-call | tf_op jit(solution)/shard_map/jit(cholesky)/cholesky | solution.py:11
  164.8 0.6 compare_reduce_fusion
  165.5 0.7 fusion.31
  166.1 9.8 %custom-call.7 = f32[1,128,128]{1,2,0:T(8,128)S(1)} custom-call(f32[1,128,128]{2,1,0:T(8,128)S(1)} %fusion.31), custom_call_target="InvertDiagBlocksLowerTriangular" | custom-call | tf_op jit(solution)/shard_map/jit(_solve_triangular)/triangular_solve | solution.py:12
  175.9 0.4 fusion.24
  176.4 5.1 %fusion.10 = f32[1024,128]{1,0:T(8,128)S(1)} fusion(f32[128,512]{1,0:T(8,128)S(1)} %fusion.24, f32[1024,1024]{0,1:T(8,128)} %copy-done.2, s32[]{:T(128)S(6)} %select_n.29, f32[512]{0:T(512)S(1)} %broadcast_multiply_fusion.4), kind=kOutput, calls=%fused_computation.15 | convolution fusion | flops 805830656 | bytes 2885636 | tf_op jit(solution)/shard_map/dot_general | solution.py:16
  181.5 0.0 copy-start.5
  181.5 0.1 copy.12
  181.7 0.0 slice-start
  181.7 0.7 convolution_convert_fusion
  182.4 0.0 copy-start.3
  182.4 0.0 slice-start.1
  182.4 0.0 slice-start.2
  182.5 0.0 slice-start.3
  182.5 8.1 %fusion.4 = f32[1024]{0:T(1024)S(1)} fusion(f32[4096]{0:T(1024)S(1)} %get-tuple-element.8, bf16[2,1024,4096]{2,1,0:T(8,128)(2,1)} %param.7, bf16[2,128,4096]{2,1,0:T(8,128)(2,1)S(1)} %convolution_convert_fusion, f32[1024,128]{1,0:T(8,128)S(1)} %fusion.10), kind=kOutput, calls=%fused_computation.8 | convolution fusion | flops 1103232000 | bytes 9981952 | tf_op jit(solution)/shard_map/dot_general | solution.py:51
  190.6 0.0 copy-done.5
  190.6 0.0 copy-done.3
  190.7 0.1 slice-done.3
  190.8 4.5 %fusion.9 = f32[1024]{0:T(1024)S(1)} fusion(f32[4096]{0:T(1024)S(1)} %get-tuple-element.7, bf16[2,1024,4096]{2,1,0:T(8,128)(2,1)S(1)} %bitcast.74, bf16[2,128,4096]{2,1,0:T(8,128)(2,1)S(1)} %convolution_convert_fusion, f32[1024,128]{1,0:T(8,128)S(1)} %fusion.10), kind=kOutput, calls=%fused_computation.13 | convolution fusion | flops 1103232000 | bytes 9981952 | tf_op jit(solution)/shard_map/dot_general | solution.py:51
  195.3 20.5 %psum.15 = f32[2,1024]{1,0:T(2,128)} all-reduce(f32[2,1024]{1,0:T(2,128)S(1)} %pad_maximum_fusion), channel_id=1, replica_groups=mesh['var'=4,'space'=8] {'space'}, use_global_device_ids=true, to_apply=%region_8.11 | all-reduce | flops 2048 | bytes 16384 | tf_op jit(solution)/shard_map/psum | solution.py:55
  (29 shorter events, 0.5 us)
Async XLA Ops:
  7.2 119.0 %copy-start = (f32[512,128]{1,0:T(8,128)S(1)}, f32[512,128]{1,0:T(8,128)}, u32[]{:S(2)}) copy-start(f32[512,128]{1,0:T(8,128)} %param.9) | copy-start | bytes 786436
  7.2 88.6 %all-reduce.2.cloned.1.call-start = ((), (), s32[]{:S(2)}) async-start(), calls=%async_computation | async-start | bytes 1048576 | tf_op jit(solution)/shard_map/psum | solution.py:27
  95.8 26.2 %copy-start.4 = (f32[1024,128]{0,1:T(8,128)S(1)}, f32[1024,128]{0,1:T(8,128)}, u32[]{:S(2)}) copy-start(f32[1024,128]{0,1:T(8,128)} %all-reduce.2.cloned.1.call-done) | copy-start | bytes 1572868
  95.8 8.8 %collective-permute-start = (f32[1024,128]{0,1:T(8,128)}, f32[1024,128]{0,1:T(8,128)S(1)}, u32[]{:S(2)}, u32[]{:S(2)}) collective-permute-start(f32[1024,128]{0,1:T(8,128)} %all-reduce.2.cloned.1.call-done), channel_id=1, source_target_pairs={{0,8},{8,16},{16,24},{24,0},{1,9},{9,17},{17,25},{25,1},{2,10},{10... | collective-permute-start | bytes 1572872 | tf_op jit(solution)/shard_map/ppermute | solution.py:32
  104.6 8.6 %collective-permute-start.1 = (f32[1024,128]{0,1:T(8,128)S(1)}, f32[1024,128]{0,1:T(8,128)S(1)}, u32[]{:S(2)}, u32[]{:S(2)}) collective-permute-start(f32[1024,128]{0,1:T(8,128)S(1)} %collective-permute-done), channel_id=1, source_target_pairs={{0,8},{8,16},{16,24},{24,0},{1,9},{9,17},{17,25},{25,1},{2,10},{10... | collective-permute-start | bytes 1572872 | tf_op jit(solution)/shard_map/ppermute | solution.py:32
  113.2 8.6 %collective-permute-start.2 = (f32[1024,128]{0,1:T(8,128)S(1)}, f32[1024,128]{0,1:T(8,128)S(1)}, u32[]{:S(2)}, u32[]{:S(2)}) collective-permute-start(f32[1024,128]{0,1:T(8,128)S(1)} %collective-permute-done.1), channel_id=1, source_target_pairs={{0,8},{8,16},{16,24},{24,0},{1,9},{9,17},{17,25},{25,1},{2,10},{10... | collective-permute-start | bytes 1572872 | tf_op jit(solution)/shard_map/ppermute | solution.py:32
  122.2 3.9 %copy-start.2 = (f32[1024,1024]{0,1:T(8,128)}, f32[1024,1024]{0,1:T(8,128)S(1)}, u32[]{:S(2)}) copy-start(f32[1024,1024]{0,1:T(8,128)S(1)} %constant_dynamic-update-slice_fusion) | copy-start | bytes 12582916
  127.1 54.5 %copy-start.1 = (bf16[2,64,4096]{2,1,0:T(8,128)(2,1)S(1)}, bf16[2,64,4096]{2,1,0:T(8,128)(2,1)}, u32[]{:S(2)}) copy-start(bf16[2,64,4096]{2,1,0:T(8,128)(2,1)} %param.8) | copy-start | bytes 3145732
  181.5 9.1 %copy-start.5 = (f32[1024,128]{1,0:T(8,128)}, f32[1024,128]{1,0:T(8,128)S(1)}, u32[]{:S(2)}) copy-start(f32[1024,128]{1,0:T(8,128)S(1)} %fusion.10) | copy-start | bytes 1572868
  181.7 9.0 %slice-start = ((s8[16777216]{0:T(1024)(128)(4,1)}), s8[4194304]{0:T(1024)(128)(4,1)S(1)}, s32[]{:S(2)}) async-start(s8[16777216]{0:T(1024)(128)(4,1)} %bitcast.73), calls=%async_computation.1 | async-start | bytes 8388608
  182.4 8.2 %copy-start.3 = (bf16[2,128,4096]{2,1,0:T(8,128)(2,1)}, bf16[2,128,4096]{2,1,0:T(8,128)(2,1)S(1)}, u32[]{:S(2)}) copy-start(bf16[2,128,4096]{2,1,0:T(8,128)(2,1)S(1)} %convolution_convert_fusion) | copy-start | bytes 6291460
  182.4 8.2 %slice-start.1 = ((s8[16777216]{0:T(1024)(128)(4,1)}), s8[4194304]{0:T(1024)(128)(4,1)S(1)}, s32[]{:S(2)}) async-start(s8[16777216]{0:T(1024)(128)(4,1)} %bitcast.73), calls=%async_computation.2 | async-start | bytes 8388608
  182.4 8.2 %slice-start.2 = ((s8[16777216]{0:T(1024)(128)(4,1)}), s8[4194304]{0:T(1024)(128)(4,1)S(1)}, s32[]{:S(2)}) async-start(s8[16777216]{0:T(1024)(128)(4,1)} %bitcast.73), calls=%async_computation.3 | async-start | bytes 8388608
  182.5 8.3 %slice-start.3 = ((s8[16777216]{0:T(1024)(128)(4,1)}), s8[4194304]{0:T(1024)(128)(4,1)S(1)}, s32[]{:S(2)}) async-start(s8[16777216]{0:T(1024)(128)(4,1)} %bitcast.73), calls=%async_computation.4 | async-start | bytes 8388608
Sparse Core Ops, SparseCore 0:
  20.3 75.4 all-reduce.1
